TPU v7x, 32 devices: a whole 2x2x4 slice. The times are simulated.
32 devices in a mesh: groups: 2 (over x), context: 16 (over z, y, core).
Axes of the slice: x: 2, y: 2, z: 4, core: 2. Of those that a mesh axis runs over, the one named last changes fastest.
Arguments:
- encoded: bfloat16 [24576, 1536], P(('groups', 'context')), parts along dimension 0, may hold values from -64 to 64, as said below
- query_weight: bfloat16 [1536, 768], P('context'), may hold values from -0.104613624 to 0.104613624
- key_weight: bfloat16 [1536, 768], P('context'), may hold values from -4 to 4
- value_weight: bfloat16 [1536, 768], P('context'), may hold values from -0.15625 to 0.15625
- out_weight: bfloat16 [1536, 768], P('context'), may hold values from -0.875 to 0.875
- cotangent: bfloat16 [24576, 1536], P(('groups', 'context')), parts along dimension 0, may hold values from -6 to 6
- valid_frames: int32 [2], P('groups'), parts along dimension 0, may hold values from 11536 to 12288
Outputs:
- layer_out: bfloat16 [24576, 1536], P(('groups', 'context')), parts along dimension 0
- encoded_grad: bfloat16 [24576, 1536], P(('groups', 'context')), parts along dimension 0
- query_weight_grad: float32 [3072, 768], P(('groups', 'context')), parts along dimension 0
- key_weight_grad: float32 [3072, 768], P(('groups', 'context')), parts along dimension 0
- value_weight_grad: float32 [3072, 768], P(('groups', 'context')), parts along dimension 0
- out_weight_grad: float32 [3072, 768], P(('groups', 'context')), parts along dimension 0
There are 2 independent parts, one for each index of `groups`. A program takes and returns all parts, laid end to end along the dimension named above; an argument that names none is the same for every part. Nothing has to cross between parts.
Inputs may be any that keep to these rules, and one draw needn't show every extreme that they name: Frames at position valid_frames and later are padding. `encoded`: drawn afresh for each recording.
All inputs are finite; a program needn't handle non-finite values.
Results may differ from a plain program's by a relative error of at most 0.014.
The roundings to bfloat16 on the way count: a program that leaves them out, or rounds other values in their place, can miss the bound.
Values may be sent and summed in bfloat16 or wider, within the bound.
No kernel may reach another device: no remote copies, remote signals or barrier semaphores. Data moves between devices by JAX's collectives and lax.ppermute only.
A program may use at most 192 MiB of HBM per device.

v0:
```python
import jax
import jax.numpy as jnp
from jax import lax
from jax.sharding import PartitionSpec as P

HEADS = 12
HD = 64
BLOCK = 16
LEFT = 16
E = 768
epsilon = 1e-05


def passed_along(value, axis, by):
    count = lax.axis_size(axis)
    pairs = [(i, i + by) for i in range(count) if 0 <= i + by < count]
    return lax.ppermute(value, axis, pairs)


def normalize(encoded):
    values = encoded.astype(jnp.float32)
    centered = values - jnp.mean(values, axis=1, keepdims=True)
    inverse = lax.rsqrt(jnp.mean(centered * centered, axis=1, keepdims=True) + epsilon)
    return (centered * inverse, inverse)


def tile_probs(query_tile, key_tile, query_first, valid_count):
    span_rows = query_tile.shape[0]
    query_pos = query_first + jnp.arange(span_rows, dtype=jnp.int32)
    key_pos = query_first - span_rows + jnp.arange(2 * span_rows, dtype=jnp.int32)
    query_block = query_pos // BLOCK
    key_block = key_pos // BLOCK
    allowed = (key_pos[None, :] >= 0) & (key_pos[None, :] < valid_count)
    allowed = (
        allowed
        & (key_block[None, :] <= query_block[:, None])
        & (key_block[None, :] >= query_block[:, None] - LEFT)
    )
    scores = jnp.einsum(
        "qhd,khd->hqk",
        query_tile.reshape(span_rows, HEADS, HD),
        key_tile.reshape(2 * span_rows, HEADS, HD),
        preferred_element_type=jnp.float32,
    ) * HD ** (-0.5)
    scores = jnp.where(allowed[None], scores, -1e30)
    row_max = jnp.max(scores, axis=2, keepdims=True)
    shifted = jnp.exp(scores - row_max)
    return shifted / jnp.sum(shifted, axis=2, keepdims=True)


def shards(encoded, query_weight, key_weight, value_weight, out_weight, cotangent, valid_frames):
    valid_count = valid_frames[0]
    frames_dev = encoded.shape[0]
    span_rows = LEFT * BLOCK
    tile_total = frames_dev // span_rows
    first_row = lax.axis_index("context") * frames_dev
    row_mask = (first_row + jnp.arange(frames_dev, dtype=jnp.int32) < valid_count).astype(
        jnp.float32
    )[:, None]
    unit_rows, inverse = normalize(encoded)
    normed = unit_rows.astype(jnp.bfloat16)
    in_weights = jnp.concatenate([query_weight, key_weight, value_weight], axis=1)
    projected = jnp.dot(
        normed,
        lax.all_gather(in_weights, "context", axis=0, tiled=True),
        preferred_element_type=jnp.float32,
    )
    projected = projected.astype(jnp.bfloat16)
    queries = projected[:, :E]
    left_kv = passed_along(projected[frames_dev - span_rows :, E:], "context", 1)
    all_kv = jnp.concatenate([left_kv, projected[:, E:]], axis=0)
    prob_tiles = []
    low_tiles = []
    mixed_tiles = []
    for tile_id in range(tile_total):
        tile_start = tile_id * span_rows
        query_tile = queries[tile_start : tile_start + span_rows]
        kv_tile = all_kv[tile_start : tile_start + 2 * span_rows]
        attn_probs = tile_probs(query_tile, kv_tile[:, :E], first_row + tile_start, valid_count)
        probs_low = attn_probs.astype(jnp.bfloat16)
        value_tile = kv_tile[:, E:].reshape(2 * span_rows, HEADS, HD)
        mixed = jnp.einsum(
            "hqk,khd->qhd", probs_low, value_tile, preferred_element_type=jnp.float32
        )
        prob_tiles.append(attn_probs)
        low_tiles.append(probs_low)
        mixed_tiles.append(mixed.reshape(span_rows, E))
    attended = (jnp.concatenate(mixed_tiles, axis=0) * row_mask).astype(jnp.bfloat16)
    cotan_cols = cotangent
    out_grad_rows = lax.psum_scatter(
        jnp.einsum("fc,fe->ce", cotan_cols, attended, preferred_element_type=jnp.float32).astype(
            jnp.bfloat16
        ),
        "context",
        scatter_dimension=0,
        tiled=True,
    ).astype(jnp.float32)
    projected_out = jnp.einsum(
        "fe,de->fd",
        attended,
        lax.all_gather(out_weight, "context", axis=0, tiled=True),
        preferred_element_type=jnp.float32,
    )
    layer_out = (encoded.astype(jnp.float32) + projected_out).astype(jnp.bfloat16)
    cotan_cols = cotangent
    grad_attn = jnp.dot(
        cotan_cols,
        lax.all_gather(out_weight, "context", axis=0, tiled=True),
        preferred_element_type=jnp.float32,
    )
    grad_attn = (grad_attn * row_mask).astype(jnp.bfloat16)
    kv_back = jnp.zeros((frames_dev + span_rows, 2 * E), jnp.float32)
    query_tiles = []
    for tile_id in range(tile_total):
        tile_start = tile_id * span_rows
        query_tile = queries[tile_start : tile_start + span_rows].reshape(span_rows, HEADS, HD)
        kv_tile = all_kv[tile_start : tile_start + 2 * span_rows]
        key_tile = kv_tile[:, :E].reshape(2 * span_rows, HEADS, HD)
        value_tile = kv_tile[:, E:].reshape(2 * span_rows, HEADS, HD)
        grad_tile = grad_attn[tile_start : tile_start + span_rows].reshape(span_rows, HEADS, HD)
        attn_probs = prob_tiles[tile_id]
        prob_grad = jnp.einsum(
            "qhd,khd->hqk", grad_tile, value_tile, preferred_element_type=jnp.float32
        )
        row_delta = jnp.sum(attn_probs * prob_grad, axis=2, keepdims=True)
        score_grad = (attn_probs * (prob_grad - row_delta) * HD ** (-0.5)).astype(jnp.bfloat16)
        query_tiles.append(
            jnp.einsum(
                "hqk,khd->qhd", score_grad, key_tile, preferred_element_type=jnp.float32
            ).reshape(span_rows, E)
        )
        key_part = jnp.einsum(
            "hqk,qhd->khd", score_grad, query_tile, preferred_element_type=jnp.float32
        ).reshape(2 * span_rows, E)
        value_part = jnp.einsum(
            "hqk,qhd->khd", low_tiles[tile_id], grad_tile, preferred_element_type=jnp.float32
        ).reshape(2 * span_rows, E)
        kv_back = kv_back.at[tile_start : tile_start + 2 * span_rows].add(
            jnp.concatenate([key_part, value_part], axis=1)
        )
    returned = passed_along(kv_back[:span_rows].astype(jnp.bfloat16), "context", -1).astype(
        jnp.float32
    )
    own_back = kv_back[span_rows:].at[frames_dev - span_rows :].add(returned)
    back_rows = jnp.concatenate([jnp.concatenate(query_tiles, axis=0), own_back], axis=1).astype(
        jnp.bfloat16
    )
    in_grad_rows = lax.psum_scatter(
        jnp.einsum("fc,fe->ce", normed, back_rows, preferred_element_type=jnp.float32).astype(
            jnp.bfloat16
        ),
        "context",
        scatter_dimension=0,
        tiled=True,
    ).astype(jnp.float32)
    feature_grad = jnp.einsum(
        "fe,de->fd",
        back_rows,
        lax.all_gather(in_weights, "context", axis=0, tiled=True),
        preferred_element_type=jnp.float32,
    )
    centered_grad = (
        feature_grad
        - jnp.mean(feature_grad, axis=1, keepdims=True)
        - unit_rows * jnp.mean(feature_grad * unit_rows, axis=1, keepdims=True)
    )
    encoded_grad = (cotangent.astype(jnp.float32) + inverse * centered_grad).astype(jnp.bfloat16)
    return (
        layer_out,
        encoded_grad,
        in_grad_rows[:, :E],
        in_grad_rows[:, E : 2 * E],
        in_grad_rows[:, 2 * E : 3 * E],
        out_grad_rows,
    )


def solution(mesh):
    placed = (
        P(("groups", "context"), None),
        P("context", None),
        P("context", None),
        P("context", None),
        P("context", None),
        P(("groups", "context"), None),
        P("groups"),
    )
    return jax.shard_map(
        shards,
        mesh=mesh,
        in_specs=placed,
        out_specs=(
            P(("groups", "context"), None),
            P(("groups", "context"), None),
            P(("groups", "context"), None),
            P(("groups", "context"), None),
            P(("groups", "context"), None),
            P(("groups", "context"), None),
        ),
        check_vma=False,
    )
```

profile of v0, /device:TPU:0, one launch (start us, length us, event | category | flops | bytes accessed | tf_op | source)
XLA Modules:
  0.0 498.0 jit_solution(1828219959673834523)
XLA Ops:
  17.7 37.5 %all-gather.5.cloned.1.call-done = bf16[1536,768]{1,0:T(8,128)(2,1)} async-done(((bf16[96,768]{1,0:T(8,128)(2,1)}), bf16[1536,768]{1,0:T(8,128)(2,1)}) %all-gather.5.cloned.1.call-update) | async-done | bytes 2359312 | tf_op jit(solution)/shard_map/all_gather | solution.py:101
  55.2 4.4 multiply_convert_fusion.3
  60.6 62.9 %all-gather.3.cloned.1.call-done = bf16[1536,2304]{1,0:T(8,128)(2,1)} async-done(((bf16[96,2304]{1,0:T(8,128)(2,1)}), bf16[1536,2304]{1,0:T(8,128)(2,1)}) %all-gather.3.cloned.1.call-update) | async-done | bytes 7077904 | tf_op jit(solution)/shard_map/all_gather | solution.py:65
  123.5 9.1 %convolution_convert_fusion.1 = bf16[768,2304]{1,0:T(8,128)(2,1)S(1)} fusion(bf16[1536,2304]{1,0:T(8,128)(2,1)} %all-gather.3.cloned.1.call-done, bf16[768,1536]{1,0:T(8,128)(2,1)S(1)} %copy-done.1, f32[768]{0:T(1024)S(1)} %add_rsqrt_fusion, f32[768]{0:T(1024)S(1)} %broadcast_multiply_fusion.2), kind=kOutput, calls=%fused_computation.32 | convolution fusion | flops 5442306048 | bytes 12982272 | tf_op jit(solution)/shard_map/dot_general | solution.py:63
  143.1 6.8 %fusion.143 = (f32[12,256]{1,0:T(8,128)}, f32[12,256,512]{2,1,0:T(8,128)}) fusion(pred[256,512]{1,0:T(8,128)(4,1)} %compare_and_fusion, bf16[256,12,64]{0,2,1:T(8,128)(2,1)} %bitcast.117, bf16[512,12,64]{0,2,1:T(8,128)(2,1)} %bitcast.109), kind=kOutput, calls=%fused_computation.187 | convolution fusion | flops 207618560 | bytes 7614464 | tf_op jit(solution)/shard_map/sub | solution.py:47
  149.9 5.1 %fusion.69 = f32[12,64,256]{2,1,0:T(8,128)} fusion(bf16[512,12,64]{0,2,1:T(8,128)(2,1)} %bitcast.93, f32[12,256,512]{2,1,0:T(8,128)} %get-tuple-element.92, f32[12,256]{1,0:T(8,128)} %get-tuple-element.91), kind=kOutput, calls=%fused_computation.81 | convolution fusion | flops 204472320 | bytes 7876608 | tf_op jit(solution)/shard_map/hqk,khd->qhd/dot_general | solution.py:82
  156.9 3.6 fusion.148
  160.5 3.3 collective-permute-start
  171.1 23.3 %fusion.43 = f32[12,64,512]{2,1,0:T(8,128)} fusion(bf16[256,12,64]{0,2,1:T(8,128)(2,1)} %bitcast.118, f32[12,256,512]{2,1,0:T(8,128)} %fusion.148, f32[12,256,512]{2,1,0:T(8,128)} %get-tuple-element.92, f32[12,256]{1,0:T(8,128)} %get-tuple-element.91), kind=kOutput, calls=%fused_computation.49 | convolution fusion | flops 212340224 | bytes 14561280 | tf_op jit(solution)/shard_map/hqk,qhd->khd/dot_general | solution.py:132
  194.4 4.7 fusion.147
  199.1 6.8 %fusion.144 = (f32[12,256]{1,0:T(8,128)}, f32[12,256,512]{2,1,0:T(8,128)}) fusion(pred[256,512]{1,0:T(8,128)(4,1)} %compare_and_fusion.1, bf16[256,12,64]{0,2,1:T(8,128)(2,1)} %bitcast.119, bf16[512,12,64]{0,2,1:T(8,128)(2,1)} %bitcast.111), kind=kOutput, calls=%fused_computation.188 | convolution fusion | flops 207618560 | bytes 7614464 | tf_op jit(solution)/shard_map/sub | solution.py:47
  205.9 4.9 fusion.73
  210.8 23.6 %fusion.37 = f32[12,64,512]{2,1,0:T(8,128)} fusion(bf16[256,12,64]{0,2,1:T(8,128)(2,1)} %bitcast.120, f32[12,256,512]{2,1,0:T(8,128)} %fusion.147, f32[12,256,512]{2,1,0:T(8,128)} %get-tuple-element.94, f32[12,256]{1,0:T(8,128)} %get-tuple-element.93), kind=kOutput, calls=%fused_computation.47 | convolution fusion | flops 212340224 | bytes 14561280 | tf_op jit(solution)/shard_map/hqk,qhd->khd/dot_general | solution.py:132
  234.5 4.9 fusion.71
  244.1 6.8 %fusion.145 = (f32[12,256]{1,0:T(8,128)}, f32[12,256,512]{2,1,0:T(8,128)}) fusion(pred[256,512]{1,0:T(8,128)(4,1)} %compare_and_fusion.2, bf16[256,12,64]{0,2,1:T(8,128)(2,1)} %bitcast.115, bf16[512,12,64]{0,2,1:T(8,128)(2,1)} %bitcast.113), kind=kOutput, calls=%fused_computation.189 | convolution fusion | flops 207618560 | bytes 7614464 | tf_op jit(solution)/shard_map/sub | solution.py:47
  250.9 5.0 fusion.77
  257.7 3.6 fusion.146
  261.4 23.3 %fusion.31 = f32[12,64,512]{2,1,0:T(8,128)} fusion(bf16[256,12,64]{0,2,1:T(8,128)(2,1)} %bitcast.116, f32[12,256,512]{2,1,0:T(8,128)} %fusion.146, f32[12,256,512]{2,1,0:T(8,128)} %get-tuple-element.96, f32[12,256]{1,0:T(8,128)} %get-tuple-element.95), kind=kOutput, calls=%fused_computation.45 | convolution fusion | flops 212340224 | bytes 14561280 | tf_op jit(solution)/shard_map/hqk,qhd->khd/dot_general | solution.py:132
  284.6 5.5 %fusion.64 = bf16[1536,768]{0,1:T(8,128)(2,1)} fusion(bf16[768,1536]{1,0:T(8,128)(2,1)} %param.20, f32[256,768]{0,1:T(8,128)S(1)} %bitcast.121, f32[256,768]{0,1:T(8,128)} %bitcast.123, f32[256,768]{0,1:T(8,128)} %bitcast.125, f32[768]{0:T(1024)S(1)} %fusion.95), kind=kOutput, calls=%fused_computation.72 | convolution fusion | flops 1815478272 | bytes 7080960 | tf_op jit(solution)/shard_map/fc,fe->ce/dot_general | solution.py:91
  290.2 4.3 copy.52
  294.8 2.8 select_maximum_fusion
  299.6 2.9 constant_dynamic-update-slice_fusion
  307.4 25.0 %fusion.79 = bf16[12,64,256]{2,1,0:T(8,128)(2,1)S(1)} fusion(bf16[512,12,64]{0,2,1:T(8,128)(2,1)S(1)} %bitcast.110, f32[12,256,512]{2,1,0:T(8,128)} %fusion.148, f32[12,256,512]{2,1,0:T(8,128)} %get-tuple-element.92, f32[12,256]{1,0:T(8,128)} %get-tuple-element.91), kind=kOutput, calls=%fused_computation.91 | convolution fusion | flops 212536832 | bytes 13774848 | tf_op jit(solution)/shard_map/hqk,khd->qhd/dot_general | solution.py:128
  332.4 22.6 %fusion.82 = bf16[12,64,256]{2,1,0:T(8,128)(2,1)} fusion(bf16[512,12,64]{0,2,1:T(8,128)(2,1)} %bitcast.112, f32[12,256,512]{2,1,0:T(8,128)} %fusion.147, f32[12,256,512]{2,1,0:T(8,128)} %get-tuple-element.94, f32[12,256]{1,0:T(8,128)} %get-tuple-element.93), kind=kOutput, calls=%fused_computation.92 | convolution fusion | flops 212536832 | bytes 13774848 | tf_op jit(solution)/shard_map/hqk,khd->qhd/dot_general | solution.py:128
  355.0 4.0 slice.196
  359.0 25.7 %fusion.85 = bf16[12,64,256]{2,1,0:T(8,128)(2,1)} fusion(bf16[512,12,64]{0,2,1:T(8,128)(2,1)S(1)} %bitcast.114, f32[12,256,512]{2,1,0:T(8,128)} %fusion.146, f32[12,256,512]{2,1,0:T(8,128)} %get-tuple-element.96, f32[12,256]{1,0:T(8,128)} %get-tuple-element.95), kind=kOutput, calls=%fused_computation.93 | convolution fusion | flops 212536832 | bytes 13774848 | tf_op jit(solution)/shard_map/hqk,khd->qhd/dot_general | solution.py:128
  384.8 2.7 fusion.66
  387.5 11.0 %convolution_convert_fusion = bf16[1536,2304]{1,0:T(8,128)(2,1)} fusion(bf16[768,1536]{0,1:T(8,128)(2,1)} %fusion.66, bf16[256,768]{0,1:T(8,128)(2,1)S(1)} %bitcast.127, bf16[256,768]{0,1:T(8,128)(2,1)} %bitcast.129, bf16[256,768]{0,1:T(8,128)(2,1)} %bitcast.131, bf16[768,1536]{1,0:T(8,128)(2,1)S(1)} %copy-done.1, f32[768]{0:T(1024)S(1)} %add_rsqrt_fusion, ...), kind=kOutput, calls=%fused_computation.6 | convolution fusion | flops 5458231296 | bytes 12982272 | tf_op jit(solution)/shard_map/fc,fe->ce/dot_general | solution.py:149
  399.6 5.7 %fusion.23 = bf16[768,1536]{1,0:T(8,128)(2,1)} fusion(bf16[768,1536]{1,0:T(8,128)(2,1)S(1)} %copy-done.1, bf16[1536,768]{1,0:T(8,128)(2,1)} %all-gather.5.cloned.1.call-done, f32[256,768]{0,1:T(8,128)S(1)} %bitcast.122, f32[256,768]{0,1:T(8,128)} %bitcast.124, f32[256,768]{0,1:T(8,128)} %bitcast.126, f32[768]{0:T(1024)S(1)} %fusion.95), kind=kOutput, calls=%fused_computation.42 | convolution fusion | flops 1817837568 | bytes 9440256 | tf_op jit(solution)/shard_map/fe,de->fd/dot_general | solution.py:98
  405.3 10.9 %fusion.138 = (f32[768]{0:T(1024)S(1)}, f32[768]{0:T(1024)S(1)}, f32[768,1536]{1,0:T(8,128)S(1)}) fusion(f32[768]{0:T(1024)S(1)} %add_rsqrt_fusion, f32[768]{0:T(1024)S(1)} %broadcast_multiply_fusion.2, bf16[768,1536]{1,0:T(8,128)(2,1)S(1)} %copy-done.1, bf16[1536,2304]{1,0:T(8,128)(2,1)} %all-gather.3.cloned.1.call-done, ...), kind=kOutput, calls=%fused_computation.182 | convolution fusion | flops 5457049600 | bytes 17707008 | tf_op jit(solution)/shard_map/fe,de->fd/dot_general | solution.py:156
  416.3 2.8 fusion.21
  421.1 68.0 %reduce-scatter.5.cloned.1.call-done = bf16[96,2304]{1,0:T(8,128)(2,1)} async-done(((bf16[1536,2304]{1,0:T(8,128)(2,1)}), bf16[96,2304]{1,0:T(8,128)(2,1)}) %reduce-scatter.5.cloned.1.call-update) | async-done | bytes 442384 | tf_op jit(solution)/shard_map/reduce_scatter | solution.py:148
  (102 shorter events, 49.0 us)
Async XLA Ops:
  7.2 48.1 %all-gather.5.cloned.1.call-start = ((), (), s32[]{:S(2)}) async-start(), calls=%async_computation.3 | async-start | bytes 2506752 | tf_op jit(solution)/shard_map/all_gather | solution.py:101
  7.9 115.6 %all-gather.3.cloned.1.call-start = ((), (), s32[]{:S(2)}) async-start(), calls=%async_computation.2 | async-start | bytes 7520256 | tf_op jit(solution)/shard_map/all_gather | solution.py:65
  9.8 409.3 %reduce-scatter.7.cloned.1.call-start = ((), (), s32[]{:S(2)}) async-start(), calls=%async_computation.5 | async-start | bytes 2506752
  17.7 105.8 %copy-start.1 = (bf16[768,1536]{1,0:T(8,128)(2,1)S(1)}, bf16[768,1536]{1,0:T(8,128)(2,1)}, u32[]{:S(2)}) copy-start(bf16[768,1536]{1,0:T(8,128)(2,1)} %param.15) | copy-start | bytes 7077892
  132.7 3.9 copy-start.2
  149.9 5.1 %copy-start.8 = (bf16[256,768]{0,1:T(8,128)(2,1)S(1)}, bf16[256,768]{0,1:T(8,128)(2,1)}, u32[]{:S(2)}) copy-start(bf16[256,768]{0,1:T(8,128)(2,1)} %get-tuple-element.85) | copy-start | bytes 1179652
  149.9 5.1 %copy-start.19 = (f32[12,256,512]{2,1,0:T(8,128)S(1)}, f32[12,256,512]{2,1,0:T(8,128)}, u32[]{:S(2)}) copy-start(f32[12,256,512]{2,1,0:T(8,128)} %get-tuple-element.92) | copy-start | bytes 18874372
  149.9 5.1 %copy-start.21 = (f32[12,256]{1,0:T(8,128)S(1)}, f32[12,256]{1,0:T(8,128)}, u32[]{:S(2)}) copy-start(f32[12,256]{1,0:T(8,128)} %get-tuple-element.91) | copy-start | bytes 36868
  155.0 1.9 copy-start.3
  160.5 78.9 %collective-permute-start = (bf16[256,1536]{1,0:T(8,128)(2,1)}, bf16[256,1536]{1,0:T(8,128)(2,1)}, u32[]{:S(2)}, u32[]{:S(2)}) collective-permute-start(bf16[256,1536]{1,0:T(8,128)(2,1)} %slice.182), channel_id=1, source_target_pairs={{0,1},{1,2},{2,3},{3,4},{4,5},{5,6},{6,7},{7,8},{8,9},{9,10},{10,1... | collective-permute-start | bytes 2359304 | tf_op jit(solution)/shard_map/ppermute | solution.py:17
  171.1 23.3 %copy-start.4 = (bf16[512,768]{0,1:T(8,128)(2,1)S(1)}, bf16[512,768]{0,1:T(8,128)(2,1)}, u32[]{:S(2)}) copy-start(bf16[512,768]{0,1:T(8,128)(2,1)} %copy.45) | copy-start | bytes 2359300
  210.8 23.6 %copy-start.7 = (bf16[256,768]{0,1:T(8,128)(2,1)S(1)}, bf16[256,768]{0,1:T(8,128)(2,1)}, u32[]{:S(2)}) copy-start(bf16[256,768]{0,1:T(8,128)(2,1)} %get-tuple-element.86) | copy-start | bytes 1179652
  210.8 23.7 %copy-start.22 = (f32[12,256]{1,0:T(8,128)S(1)}, f32[12,256]{1,0:T(8,128)}, u32[]{:S(2)}) copy-start(f32[12,256]{1,0:T(8,128)} %get-tuple-element.93) | copy-start | bytes 36868
  234.5 4.9 slice-start
  250.9 5.0 copy-start.20
  250.9 5.0 copy-start.23
  261.4 23.3 %copy-start.15 = (f32[12,64,256]{2,1,0:T(8,128)S(1)}, f32[12,64,256]{2,1,0:T(8,128)}, u32[]{:S(2)}) copy-start(f32[12,64,256]{2,1,0:T(8,128)} %fusion.69) | copy-start | bytes 2359300
  294.5 194.5 %reduce-scatter.5.cloned.1.call-start = ((), (), s32[]{:S(2)}) async-start(), calls=%async_computation.4 | async-start | bytes 7520256 | tf_op jit(solution)/shard_map/reduce_scatter | solution.py:148
  294.8 2.8 copy-start.11
  294.8 2.8 copy-start.12
  297.6 1.5 copy-start.9
  297.6 2.0 copy-start.10
  299.6 7.8 %copy-start.13 = (bf16[512,768]{0,1:T(8,128)(2,1)S(1)}, bf16[512,768]{0,1:T(8,128)(2,1)}, u32[]{:S(2)}) copy-start(bf16[512,768]{0,1:T(8,128)(2,1)} %copy.50) | copy-start | bytes 2359300
  302.5 2.6 copy-start
  306.1 78.7 %collective-permute-start.1 = (bf16[256,1536]{0,1:T(8,128)(2,1)}, bf16[256,1536]{0,1:T(8,128)(2,1)}, u32[]{:S(2)}, u32[]{:S(2)}) collective-permute-start(bf16[256,1536]{0,1:T(8,128)(2,1)} %slice.210), channel_id=1, source_target_pairs={{1,0},{2,1},{3,2},{4,3},{5,4},{6,5},{7,6},{8,7},{9,8},{10,9},{11,1... | collective-permute-start | bytes 2359304 | tf_op jit(solution)/shard_map/ppermute | solution.py:17
  332.4 26.7 %copy-start.14 = (bf16[512,768]{0,1:T(8,128)(2,1)S(1)}, bf16[512,768]{0,1:T(8,128)(2,1)}, u32[]{:S(2)}) copy-start(bf16[512,768]{0,1:T(8,128)(2,1)} %copy.44) | copy-start | bytes 2359300
  398.4 1.1 copy-start.16
  399.6 5.8 %copy-start.5 = (bf16[768,1536]{0,1:T(8,128)(2,1)S(1)}, bf16[768,1536]{0,1:T(8,128)(2,1)}, u32[]{:S(2)}) copy-start(bf16[768,1536]{0,1:T(8,128)(2,1)} %fusion.66) | copy-start | bytes 7077892
  399.6 5.8 %copy-start.17 = (bf16[12,64,256]{2,1,0:T(8,128)(2,1)S(1)}, bf16[12,64,256]{2,1,0:T(8,128)(2,1)}, u32[]{:S(2)}) copy-start(bf16[12,64,256]{2,1,0:T(8,128)(2,1)} %fusion.82) | copy-start | bytes 1179652
  399.6 5.8 %copy-start.18 = (bf16[12,64,256]{2,1,0:T(8,128)(2,1)S(1)}, bf16[12,64,256]{2,1,0:T(8,128)(2,1)}, u32[]{:S(2)}) copy-start(bf16[12,64,256]{2,1,0:T(8,128)(2,1)} %fusion.85) | copy-start | bytes 1179652
  405.3 11.0 %copy-start.6 = (bf16[768,1536]{1,0:T(8,128)(2,1)S(1)}, bf16[768,1536]{1,0:T(8,128)(2,1)}, u32[]{:S(2)}) copy-start(bf16[768,1536]{1,0:T(8,128)(2,1)} %param.20) | copy-start | bytes 7077892
Sparse Core Ops, SparseCore 0:
  10.3 44.9 all-gather.4
  58.1 65.3 all-gather.2
  294.7 62.3 reduce-scatter.6
  398.6 90.4 reduce-scatter.4
where the time goes:
time: 507 us; the launch traced here: 498 us
  matrix products  246 us (49%)
  waiting for transfers between devices  169 us (33%)
  local copies, waits for them, and re-layouts  39.2 us (8%)
  other arithmetic  23.3 us (5%)
  between operations  15.2 us (3%)
    dot_general x3, matrix products, shards(): jnp.einsum('hqk,khd->qhd', score_grad, key_tile, preferred_element_type=j...  73.4 us
    dot_general x3, matrix products, shards(): jnp.einsum('hqk,qhd->khd', score_grad, query_tile, preferred_element_type...  70.2 us
    reduce_scatter x1, waiting for transfers between devices, shards(): lax.psum_scatter(jnp.einsum('fc,fe->ce', normed, back_rows, preferred_ele...  68 us
    all_gather x1, waiting for transfers between devices, shards(): lax.all_gather(in_weights, 'context', axis=0, tiled=True)  62.9 us
    all_gather x1, waiting for transfers between devices, shards(): lax.all_gather(out_weight, 'context', axis=0, tiled=True)  37.5 us
    sub x3, matrix products, tile_probs(): shifted = jnp.exp(scores - row_max)  20.4 us
    dot_general x3, matrix products, shards(): jnp.einsum('hqk,khd->qhd', probs_low, value_tile, preferred_element_type=...  15 us
    dot_general x3, matrix products, shards(): jnp.einsum('qhd,khd->hqk', grad_tile, value_tile, preferred_element_type=...  12 us
  transfers between devices with their start and end apart: 6, of which 3 were waited for; matrix products, arithmetic and copies ran while one was open for 42% of the time, Pallas kernels for 0%

commit v1 on v0

--- a/solution.py
+++ b/solution.py
@@ -9,6 +9,28 @@
 LEFT = 16
 E = 768
 epsilon = 1e-05
+
+
+def laid_out(tiles, dim):
+    tiles = jnp.moveaxis(tiles, 0, dim)
+    shape = tiles.shape
+    return tiles.reshape(*shape[:dim], shape[dim] * shape[dim + 1], *shape[dim + 2 :])
+
+
+def collect(x, axis, dim):
+    size = lax.axis_size(axis)
+    pairs = [(i, (i + 1) % size) for i in range(size)]
+    back = [(b, a) for a, b in pairs]
+    lower, upper = ([], [])
+    for lap in range(size - 1):
+        if lap % 2 == 0:
+            lower.append(lax.ppermute(lower[-1] if lower else x, axis, pairs))
+        else:
+            upper.append(lax.ppermute(upper[-1] if upper else x, axis, back))
+    blocks = jnp.stack([*lower[::-1], x, *upper])
+    shift = lax.axis_index(axis) - len(lower)
+    blocks = blocks[(jnp.arange(size) - shift) % size]
+    return laid_out(blocks, dim)
 
 
 def passed_along(value, axis, by):
@@ -61,9 +83,7 @@
     normed = unit_rows.astype(jnp.bfloat16)
     in_weights = jnp.concatenate([query_weight, key_weight, value_weight], axis=1)
     projected = jnp.dot(
-        normed,
-        lax.all_gather(in_weights, "context", axis=0, tiled=True),
-        preferred_element_type=jnp.float32,
+        normed, collect(in_weights, "context", 0), preferred_element_type=jnp.float32
     )
     projected = projected.astype(jnp.bfloat16)
     queries = projected[:, :E]

time: 507 us -> 510 us (level)
  waiting for transfers between devices: 169 us -> 117 us
  starting transfers between devices: 4.9 us -> 50.8 us
  local copies, waits for them, and re-layouts: 39.2 us -> 57.3 us
    all_gather x1, waiting for transfers between devices: 62.9 us -> 0.01 us  [shards(): lax.all_gather(in_weights, 'context', axis=0, tiled=True)]
    ppermute x0 -> x15, waiting for transfers between devices: none -> 45.9 us  [the longest x8 45.8 us: collect(): lower.append(lax.ppermute(lower[-1] if lower else x, axis, pairs))]
    ppermute x0 -> x15, starting transfers between devices: none -> 38.5 us  [the longest x8 20.1 us: collect(): lower.append(lax.ppermute(lower[-1] if lower else x, axis, pairs))]
    all_gather x1, waiting for transfers between devices: 37.5 us -> 0.02 us  [shards(): lax.all_gather(out_weight, 'context', axis=0, tiled=True)]
    unnamed x51 -> x72, local copies, waits for them, and re-layouts: 11 us -> 22.4 us
    ppermute x2, starting transfers between devices: 4.57 us -> 12.2 us  [passed_along(): return lax.ppermute(value, axis, pairs)]
    gather x0 -> x1, local copies, waits for them, and re-layouts: none -> 7.11 us  [collect(): blocks = blocks[(jnp.arange(size) - shift) % size]]
  transfers between devices with their start and end apart: 6 -> 21, of which waited for: 3 -> 9; matrix products, arithmetic and copies ran while one was open for 42% -> 62% of each run, Pallas kernels for 0% -> 0%
where the time goes in v1:
time: 510 us; the launch traced here: 504 us
  matrix products  244 us (48%)
  waiting for transfers between devices  117 us (23%)
  local copies, waits for them, and re-layouts  57.3 us (11%)
  starting transfers between devices  50.8 us (10%)
  other arithmetic  19.7 us (4%)
  between operations  15.1 us (3%)
    dot_general x3, matrix products, shards(): jnp.einsum('hqk,khd->qhd', score_grad, key_tile, preferred_element_type=j...  73.4 us
    dot_general x3, matrix products, shards(): jnp.einsum('hqk,qhd->khd', score_grad, query_tile, preferred_element_type...  70.4 us
    reduce_scatter x1, waiting for transfers between devices, shards(): lax.psum_scatter(jnp.einsum('fc,fe->ce', normed, back_rows, preferred_ele...  70.1 us
    ppermute x8, waiting for transfers between devices, collect(): lower.append(lax.ppermute(lower[-1] if lower else x, axis, pairs))  45.8 us
    unnamed x72, local copies, waits for them, and re-layouts  22.4 us
    sub x3, matrix products, tile_probs(): shifted = jnp.exp(scores - row_max)  20.1 us
    ppermute x8, starting transfers between devices, collect(): lower.append(lax.ppermute(lower[-1] if lower else x, axis, pairs))  20.1 us
    ppermute x7, starting transfers between devices, collect(): upper.append(lax.ppermute(upper[-1] if upper else x, axis, back))  18.4 us
  transfers between devices with their start and end apart: 21, of which 9 were waited for; matrix products, arithmetic and copies ran while one was open for 62% of the time, Pallas kernels for 0%

profile of v1, /device:TPU:0, one launch (start us, length us, event | category | flops | bytes accessed | tf_op | source)
XLA Modules:
  0.0 503.6 jit_solution(8810971154490134376)
XLA Ops:
  10.5 11.0 %collective-permute-done = bf16[96,2304]{1,0:T(8,128)(2,1)S(1)} collective-permute-done((bf16[96,2304]{1,0:T(8,128)(2,1)S(1)}, bf16[96,2304]{1,0:T(8,128)(2,1)S(1)}, u32[]{:S(2)}, u32[]{:S(2)}) %collective-permute-start) | collective-permute-done | bytes 442400 | tf_op jit(solution)/shard_map/ppermute | solution.py:27
  21.5 4.4 collective-permute-start.8
  26.7 5.3 %collective-permute-done.1 = bf16[96,2304]{1,0:T(8,128)(2,1)S(1)} collective-permute-done((bf16[96,2304]{1,0:T(8,128)(2,1)S(1)}, bf16[96,2304]{1,0:T(8,128)(2,1)S(1)}, u32[]{:S(2)}, u32[]{:S(2)}) %collective-permute-start.1) | collective-permute-done | bytes 442400 | tf_op jit(solution)/shard_map/ppermute | solution.py:27
  32.1 4.5 collective-permute-start.9
  36.6 10.1 %collective-permute-done.2 = bf16[96,2304]{1,0:T(8,128)(2,1)S(1)} collective-permute-done((bf16[96,2304]{1,0:T(8,128)(2,1)S(1)}, bf16[96,2304]{1,0:T(8,128)(2,1)S(1)}, u32[]{:S(2)}, u32[]{:S(2)}) %collective-permute-start.2) | collective-permute-done | bytes 442400 | tf_op jit(solution)/shard_map/ppermute | solution.py:27
  46.8 4.5 collective-permute-start.10
  51.2 6.2 %collective-permute-done.3 = bf16[96,2304]{1,0:T(8,128)(2,1)S(1)} collective-permute-done((bf16[96,2304]{1,0:T(8,128)(2,1)S(1)}, bf16[96,2304]{1,0:T(8,128)(2,1)S(1)}, u32[]{:S(2)}, u32[]{:S(2)}) %collective-permute-start.3) | collective-permute-done | bytes 442400 | tf_op jit(solution)/shard_map/ppermute | solution.py:27
  57.4 4.3 collective-permute-start.4
  68.4 4.5 collective-permute-start.5
  81.0 4.4 collective-permute-start.6
  91.5 6.4 %collective-permute-start.7 = (bf16[96,2304]{1,0:T(8,128)(2,1)S(1)}, bf16[96,2304]{1,0:T(8,128)(2,1)S(1)}, u32[]{:S(2)}, u32[]{:S(2)}) collective-permute-start(bf16[96,2304]{1,0:T(8,128)(2,1)S(1)} %collective-permute-done.6), channel_id=1, source_target_pairs={{0,1},{1,2},{2,3},{3,4},{4,5},{5,6},{6,7},{7,8},{8,9},{9,10},{10,1... | collective-permute-start | bytes 1327112 | tf_op jit(solution)/shard_map/ppermute | solution.py:27
  115.2 7.1 %gather_fusion = bf16[16,96,2304]{2,1,0:T(8,128)(2,1)} fusion(bf16[16,96,2304]{2,1,0:T(8,128)(2,1)} %bitcast_dynamic-update-slice_fusion, s32[1024]{0:T(1024)S(1)} %pad_clamp_fusion), kind=kCustom, calls=%fused_computation | custom fusion | bytes 14155840 | tf_op jit(solution)/shard_map/gather | solution.py:32
  122.3 9.1 %convolution_convert_fusion.1 = bf16[768,2304]{1,0:T(8,128)(2,1)S(1)} fusion(bf16[1536,2304]{1,0:T(8,128)(2,1)} %bitcast.126, bf16[768,1536]{1,0:T(8,128)(2,1)S(1)} %copy-done, f32[768]{0:T(1024)S(1)} %add_rsqrt_fusion, f32[768]{0:T(1024)S(1)} %broadcast_multiply_fusion.2), kind=kOutput, calls=%fused_computation.33 | convolution fusion | flops 5442306048 | bytes 12982272 | tf_op jit(solution)/shard_map/dot_general | solution.py:85
  135.2 10.9 %collective-permute-start.15 = (bf16[256,1536]{1,0:T(8,128)(2,1)}, bf16[256,1536]{1,0:T(8,128)(2,1)}, u32[]{:S(2)}, u32[]{:S(2)}) collective-permute-start(bf16[256,1536]{1,0:T(8,128)(2,1)} %slice.184), channel_id=1, source_target_pairs={{0,1},{1,2},{2,3},{3,4},{4,5},{5,6},{6,7},{7,8},{8,9},{9,10},{10,1... | collective-permute-start | bytes 2359304 | tf_op jit(solution)/shard_map/ppermute | solution.py:39
  158.1 6.7 %fusion.145 = (f32[12,256]{1,0:T(8,128)}, f32[12,256,512]{2,1,0:T(8,128)}) fusion(pred[256,512]{1,0:T(8,128)(4,1)} %compare_and_fusion, bf16[256,12,64]{0,2,1:T(8,128)(2,1)} %bitcast.155, bf16[512,12,64]{0,2,1:T(8,128)(2,1)} %bitcast.147), kind=kOutput, calls=%fused_computation.213 | convolution fusion | flops 207618560 | bytes 7614464 | tf_op jit(solution)/shard_map/sub | solution.py:69
  164.8 6.7 %fusion.146 = (f32[12,256]{1,0:T(8,128)}, f32[12,256,512]{2,1,0:T(8,128)}) fusion(pred[256,512]{1,0:T(8,128)(4,1)} %compare_and_fusion.1, bf16[256,12,64]{0,2,1:T(8,128)(2,1)S(1)} %bitcast.154, bf16[512,12,64]{0,2,1:T(8,128)(2,1)} %bitcast.145), kind=kOutput, calls=%fused_computation.214 | convolution fusion | flops 207618560 | bytes 7614464 | tf_op jit(solution)/shard_map/sub | solution.py:69
  171.5 5.2 %fusion.69 = f32[12,64,256]{2,1,0:T(8,128)} fusion(bf16[512,12,64]{0,2,1:T(8,128)(2,1)} %bitcast.129, f32[12,256,512]{2,1,0:T(8,128)} %get-tuple-element.92, f32[12,256]{1,0:T(8,128)} %get-tuple-element.91), kind=kOutput, calls=%fused_computation.82 | convolution fusion | flops 204472320 | bytes 7876608 | tf_op jit(solution)/shard_map/hqk,khd->qhd/dot_general | solution.py:102
  186.1 6.7 %fusion.147 = (f32[12,256]{1,0:T(8,128)}, f32[12,256,512]{2,1,0:T(8,128)}) fusion(pred[256,512]{1,0:T(8,128)(4,1)} %compare_and_fusion.2, bf16[256,12,64]{0,2,1:T(8,128)(2,1)S(1)} %bitcast.152, bf16[512,12,64]{0,2,1:T(8,128)(2,1)} %bitcast.149), kind=kOutput, calls=%fused_computation.215 | convolution fusion | flops 207618560 | bytes 7614464 | tf_op jit(solution)/shard_map/sub | solution.py:69
  206.3 4.5 multiply_convert_fusion.3
  215.4 23.8 %fusion.43 = f32[12,64,512]{2,1,0:T(8,128)} fusion(bf16[256,12,64]{0,2,1:T(8,128)(2,1)} %bitcast.156, f32[12,256,512]{2,1,0:T(8,128)} %fusion.150, f32[12,256,512]{2,1,0:T(8,128)} %get-tuple-element.92, f32[12,256]{1,0:T(8,128)} %get-tuple-element.91), kind=kOutput, calls=%fused_computation.50 | convolution fusion | flops 212340224 | bytes 14561280 | tf_op jit(solution)/shard_map/hqk,qhd->khd/dot_general | solution.py:152
  239.2 5.0 fusion.148
  244.2 23.3 %fusion.31 = f32[12,64,512]{2,1,0:T(8,128)} fusion(bf16[256,12,64]{0,2,1:T(8,128)(2,1)} %bitcast.151, f32[12,256,512]{2,1,0:T(8,128)} %fusion.148, f32[12,256,512]{2,1,0:T(8,128)} %get-tuple-element.96, f32[12,256]{1,0:T(8,128)} %get-tuple-element.95), kind=kOutput, calls=%fused_computation.46 | convolution fusion | flops 212340224 | bytes 14561280 | tf_op jit(solution)/shard_map/hqk,qhd->khd/dot_general | solution.py:152
  267.5 4.7 fusion.149
  272.2 23.2 %fusion.37 = f32[12,64,512]{2,1,0:T(8,128)} fusion(bf16[256,12,64]{0,2,1:T(8,128)(2,1)} %bitcast.153, f32[12,256,512]{2,1,0:T(8,128)} %fusion.149, f32[12,256,512]{2,1,0:T(8,128)} %get-tuple-element.94, f32[12,256]{1,0:T(8,128)} %get-tuple-element.93), kind=kOutput, calls=%fused_computation.48 | convolution fusion | flops 212340224 | bytes 14561280 | tf_op jit(solution)/shard_map/hqk,qhd->khd/dot_general | solution.py:152
  300.0 4.8 fusion.71
  314.4 24.9 %fusion.79 = bf16[12,64,256]{2,1,0:T(8,128)(2,1)S(1)} fusion(bf16[512,12,64]{0,2,1:T(8,128)(2,1)S(1)} %bitcast.148, f32[12,256,512]{2,1,0:T(8,128)} %fusion.150, f32[12,256,512]{2,1,0:T(8,128)} %get-tuple-element.92, f32[12,256]{1,0:T(8,128)} %get-tuple-element.91), kind=kOutput, calls=%fused_computation.92 | convolution fusion | flops 212536832 | bytes 13774848 | tf_op jit(solution)/shard_map/hqk,khd->qhd/dot_general | solution.py:148
  339.3 22.7 %fusion.85 = bf16[12,64,256]{2,1,0:T(8,128)(2,1)} fusion(bf16[512,12,64]{0,2,1:T(8,128)(2,1)} %bitcast.150, f32[12,256,512]{2,1,0:T(8,128)} %fusion.148, f32[12,256,512]{2,1,0:T(8,128)} %get-tuple-element.96, f32[12,256]{1,0:T(8,128)} %get-tuple-element.95), kind=kOutput, calls=%fused_computation.94 | convolution fusion | flops 212536832 | bytes 13774848 | tf_op jit(solution)/shard_map/hqk,khd->qhd/dot_general | solution.py:148
  362.1 25.7 %fusion.82 = bf16[12,64,256]{2,1,0:T(8,128)(2,1)} fusion(bf16[512,12,64]{0,2,1:T(8,128)(2,1)S(1)} %bitcast.146, f32[12,256,512]{2,1,0:T(8,128)} %fusion.149, f32[12,256,512]{2,1,0:T(8,128)} %get-tuple-element.94, f32[12,256]{1,0:T(8,128)} %get-tuple-element.93), kind=kOutput, calls=%fused_computation.93 | convolution fusion | flops 212536832 | bytes 13774848 | tf_op jit(solution)/shard_map/hqk,khd->qhd/dot_general | solution.py:148
  390.5 11.0 %convolution_convert_fusion = bf16[1536,2304]{1,0:T(8,128)(2,1)} fusion(bf16[768,1536]{0,1:T(8,128)(2,1)} %fusion.66, bf16[256,768]{0,1:T(8,128)(2,1)S(1)} %bitcast.163, bf16[256,768]{0,1:T(8,128)(2,1)} %bitcast.167, bf16[256,768]{0,1:T(8,128)(2,1)} %bitcast.165, bf16[768,1536]{1,0:T(8,128)(2,1)S(1)} %copy-done, f32[768]{0:T(1024)S(1)} %add_rsqrt_fusion, ...), kind=kOutput, calls=%fused_computation.7 | convolution fusion | flops 5458231296 | bytes 12982272 | tf_op jit(solution)/shard_map/fc,fe->ce/dot_general | solution.py:169
  402.6 5.6 %fusion.23 = bf16[768,1536]{1,0:T(8,128)(2,1)} fusion(bf16[768,1536]{1,0:T(8,128)(2,1)S(1)} %copy-done, bf16[1536,768]{1,0:T(8,128)(2,1)} %all-gather.3.cloned.1.call-done, f32[256,768]{0,1:T(8,128)S(1)} %bitcast.158, f32[256,768]{0,1:T(8,128)} %bitcast.159, f32[256,768]{0,1:T(8,128)} %bitcast.162, f32[768]{0:T(1024)S(1)} %fusion.95), kind=kOutput, calls=%fused_computation.43 | convolution fusion | flops 1817837568 | bytes 9440256 | tf_op jit(solution)/shard_map/fe,de->fd/dot_general | solution.py:118
  410.2 11.7 %fusion.140 = (f32[768]{0:T(1024)S(1)}, f32[768]{0:T(1024)S(1)}, f32[768,1536]{1,0:T(8,128)S(1)}) fusion(f32[768]{0:T(1024)S(1)} %add_rsqrt_fusion, f32[768]{0:T(1024)S(1)} %broadcast_multiply_fusion.2, bf16[768,1536]{1,0:T(8,128)(2,1)S(1)} %copy-done, bf16[1536,2304]{1,0:T(8,128)(2,1)} %all-gather.5.cloned.1.call-done, bf16[768,1536]{0,1:T(8,128)(2,1)} %fusion.66, ...), kind=kOutput, calls=%fused_computation.208 | convolution fusion | flops 5457049600 | bytes 17707008 | tf_op jit(solution)/shard_map/fe,de->fd/dot_general | solution.py:176
  424.8 70.1 %reduce-scatter.5.cloned.1.call-done = bf16[96,2304]{1,0:T(8,128)(2,1)} async-done(((bf16[1536,2304]{1,0:T(8,128)(2,1)}), bf16[96,2304]{1,0:T(8,128)(2,1)}) %reduce-scatter.5.cloned.1.call-update) | async-done | bytes 442384 | tf_op jit(solution)/shard_map/reduce_scatter | solution.py:168
  (158 shorter events, 109.4 us)
Async XLA Ops:
  7.2 199.1 %all-gather.3.cloned.1.call-start = ((), (), s32[]{:S(2)}) async-start(), calls=%async_computation.2 | async-start | bytes 2506752 | tf_op jit(solution)/shard_map/all_gather | solution.py:121
  10.0 99.6 %copy-start.3 = (bf16[96,2304]{1,0:T(8,128)(2,1)}, bf16[96,2304]{1,0:T(8,128)(2,1)S(1)}, u32[]{:S(2)}) copy-start(bf16[96,2304]{1,0:T(8,128)(2,1)S(1)} %constant_dynamic-update-slice_fusion) | copy-start | bytes 1327108
  10.0 11.5 %collective-permute-start = (bf16[96,2304]{1,0:T(8,128)(2,1)S(1)}, bf16[96,2304]{1,0:T(8,128)(2,1)S(1)}, u32[]{:S(2)}, u32[]{:S(2)}) collective-permute-start(bf16[96,2304]{1,0:T(8,128)(2,1)S(1)} %constant_dynamic-update-slice_fusion), channel_id=1, source_target_pairs={{0,1},{1,2},{2,3},{3,4},{4,5},{5,6},{6,7},{7,8},{8,9},{9,10},{10,1... | collective-permute-start | bytes 1327112 | tf_op jit(solution)/shard_map/ppermute | solution.py:27
  21.5 10.5 %collective-permute-start.1 = (bf16[96,2304]{1,0:T(8,128)(2,1)S(1)}, bf16[96,2304]{1,0:T(8,128)(2,1)S(1)}, u32[]{:S(2)}, u32[]{:S(2)}) collective-permute-start(bf16[96,2304]{1,0:T(8,128)(2,1)S(1)} %collective-permute-done), channel_id=1, source_target_pairs={{0,1},{1,2},{2,3},{3,4},{4,5},{5,6},{6,7},{7,8},{8,9},{9,10},{10,1... | collective-permute-start | bytes 1327112 | tf_op jit(solution)/shard_map/ppermute | solution.py:27
  21.5 10.6 %collective-permute-start.8 = (bf16[96,2304]{1,0:T(8,128)(2,1)S(1)}, bf16[96,2304]{1,0:T(8,128)(2,1)S(1)}, u32[]{:S(2)}, u32[]{:S(2)}) collective-permute-start(bf16[96,2304]{1,0:T(8,128)(2,1)S(1)} %constant_dynamic-update-slice_fusion), channel_id=1, source_target_pairs={{1,0},{2,1},{3,2},{4,3},{5,4},{6,5},{7,6},{8,7},{9,8},{10,9},{11,1... | collective-permute-start | bytes 1327112 | tf_op jit(solution)/shard_map/ppermute | solution.py:29
  25.9 382.3 %reduce-scatter.7.cloned.1.call-start = ((), (), s32[]{:S(2)}) async-start(), calls=%async_computation.5 | async-start | bytes 2506752
  32.0 14.7 %collective-permute-start.2 = (bf16[96,2304]{1,0:T(8,128)(2,1)S(1)}, bf16[96,2304]{1,0:T(8,128)(2,1)S(1)}, u32[]{:S(2)}, u32[]{:S(2)}) collective-permute-start(bf16[96,2304]{1,0:T(8,128)(2,1)S(1)} %collective-permute-done.1), channel_id=1, source_target_pairs={{0,1},{1,2},{2,3},{3,4},{4,5},{5,6},{6,7},{7,8},{8,9},{9,10},{10,1... | collective-permute-start | bytes 1327112 | tf_op jit(solution)/shard_map/ppermute | solution.py:27
  32.1 14.7 %collective-permute-start.9 = (bf16[96,2304]{1,0:T(8,128)(2,1)S(1)}, bf16[96,2304]{1,0:T(8,128)(2,1)S(1)}, u32[]{:S(2)}, u32[]{:S(2)}) collective-permute-start(bf16[96,2304]{1,0:T(8,128)(2,1)S(1)} %collective-permute-done.8), channel_id=1, source_target_pairs={{1,0},{2,1},{3,2},{4,3},{5,4},{6,5},{7,6},{8,7},{9,8},{10,9},{11,1... | collective-permute-start | bytes 1327112 | tf_op jit(solution)/shard_map/ppermute | solution.py:29
  46.7 10.7 %collective-permute-start.3 = (bf16[96,2304]{1,0:T(8,128)(2,1)S(1)}, bf16[96,2304]{1,0:T(8,128)(2,1)S(1)}, u32[]{:S(2)}, u32[]{:S(2)}) collective-permute-start(bf16[96,2304]{1,0:T(8,128)(2,1)S(1)} %collective-permute-done.2), channel_id=1, source_target_pairs={{0,1},{1,2},{2,3},{3,4},{4,5},{5,6},{6,7},{7,8},{8,9},{9,10},{10,1... | collective-permute-start | bytes 1327112 | tf_op jit(solution)/shard_map/ppermute | solution.py:27
  46.8 17.9 %collective-permute-start.10 = (bf16[96,2304]{1,0:T(8,128)(2,1)S(1)}, bf16[96,2304]{1,0:T(8,128)(2,1)S(1)}, u32[]{:S(2)}, u32[]{:S(2)}) collective-permute-start(bf16[96,2304]{1,0:T(8,128)(2,1)S(1)} %collective-permute-done.9), channel_id=1, source_target_pairs={{1,0},{2,1},{3,2},{4,3},{5,4},{6,5},{7,6},{8,7},{9,8},{10,9},{11,1... | collective-permute-start | bytes 1327112 | tf_op jit(solution)/shard_map/ppermute | solution.py:29
  57.4 11.0 %collective-permute-start.4 = (bf16[96,2304]{1,0:T(8,128)(2,1)S(1)}, bf16[96,2304]{1,0:T(8,128)(2,1)S(1)}, u32[]{:S(2)}, u32[]{:S(2)}) collective-permute-start(bf16[96,2304]{1,0:T(8,128)(2,1)S(1)} %collective-permute-done.3), channel_id=1, source_target_pairs={{0,1},{1,2},{2,3},{3,4},{4,5},{5,6},{6,7},{7,8},{8,9},{9,10},{10,1... | collective-permute-start | bytes 1327112 | tf_op jit(solution)/shard_map/ppermute | solution.py:27
  64.6 9.1 %collective-permute-start.11 = (bf16[96,2304]{1,0:T(8,128)(2,1)S(1)}, bf16[96,2304]{1,0:T(8,128)(2,1)S(1)}, u32[]{:S(2)}, u32[]{:S(2)}) collective-permute-start(bf16[96,2304]{1,0:T(8,128)(2,1)S(1)} %collective-permute-done.10), channel_id=1, source_target_pairs={{1,0},{2,1},{3,2},{4,3},{5,4},{6,5},{7,6},{8,7},{9,8},{10,9},{11,1... | collective-permute-start | bytes 1327112 | tf_op jit(solution)/shard_map/ppermute | solution.py:29
  68.4 12.6 %collective-permute-start.5 = (bf16[96,2304]{1,0:T(8,128)(2,1)S(1)}, bf16[96,2304]{1,0:T(8,128)(2,1)S(1)}, u32[]{:S(2)}, u32[]{:S(2)}) collective-permute-start(bf16[96,2304]{1,0:T(8,128)(2,1)S(1)} %collective-permute-done.4), channel_id=1, source_target_pairs={{0,1},{1,2},{2,3},{3,4},{4,5},{5,6},{6,7},{7,8},{8,9},{9,10},{10,1... | collective-permute-start | bytes 1327112 | tf_op jit(solution)/shard_map/ppermute | solution.py:27
  73.7 14.1 %collective-permute-start.12 = (bf16[96,2304]{1,0:T(8,128)(2,1)S(1)}, bf16[96,2304]{1,0:T(8,128)(2,1)S(1)}, u32[]{:S(2)}, u32[]{:S(2)}) collective-permute-start(bf16[96,2304]{1,0:T(8,128)(2,1)S(1)} %collective-permute-done.11), channel_id=1, source_target_pairs={{1,0},{2,1},{3,2},{4,3},{5,4},{6,5},{7,6},{8,7},{9,8},{10,9},{11,1... | collective-permute-start | bytes 1327112 | tf_op jit(solution)/shard_map/ppermute | solution.py:29
  81.0 10.4 %collective-permute-start.6 = (bf16[96,2304]{1,0:T(8,128)(2,1)S(1)}, bf16[96,2304]{1,0:T(8,128)(2,1)S(1)}, u32[]{:S(2)}, u32[]{:S(2)}) collective-permute-start(bf16[96,2304]{1,0:T(8,128)(2,1)S(1)} %collective-permute-done.5), channel_id=1, source_target_pairs={{0,1},{1,2},{2,3},{3,4},{4,5},{5,6},{6,7},{7,8},{8,9},{9,10},{10,1... | collective-permute-start | bytes 1327112 | tf_op jit(solution)/shard_map/ppermute | solution.py:27
  87.8 10.9 %collective-permute-start.13 = (bf16[96,2304]{1,0:T(8,128)(2,1)S(1)}, bf16[96,2304]{1,0:T(8,128)(2,1)S(1)}, u32[]{:S(2)}, u32[]{:S(2)}) collective-permute-start(bf16[96,2304]{1,0:T(8,128)(2,1)S(1)} %collective-permute-done.12), channel_id=1, source_target_pairs={{1,0},{2,1},{3,2},{4,3},{5,4},{6,5},{7,6},{8,7},{9,8},{10,9},{11,1... | collective-permute-start | bytes 1327112 | tf_op jit(solution)/shard_map/ppermute | solution.py:29
  91.5 10.9 %collective-permute-start.7 = (bf16[96,2304]{1,0:T(8,128)(2,1)S(1)}, bf16[96,2304]{1,0:T(8,128)(2,1)S(1)}, u32[]{:S(2)}, u32[]{:S(2)}) collective-permute-start(bf16[96,2304]{1,0:T(8,128)(2,1)S(1)} %collective-permute-done.6), channel_id=1, source_target_pairs={{0,1},{1,2},{2,3},{3,4},{4,5},{5,6},{6,7},{7,8},{8,9},{9,10},{10,1... | collective-permute-start | bytes 1327112 | tf_op jit(solution)/shard_map/ppermute | solution.py:27
  98.7 15.7 %collective-permute-start.14 = (bf16[96,2304]{1,0:T(8,128)(2,1)S(1)}, bf16[96,2304]{1,0:T(8,128)(2,1)S(1)}, u32[]{:S(2)}, u32[]{:S(2)}) collective-permute-start(bf16[96,2304]{1,0:T(8,128)(2,1)S(1)} %collective-permute-done.13), channel_id=1, source_target_pairs={{1,0},{2,1},{3,2},{4,3},{5,4},{6,5},{7,6},{8,7},{9,8},{10,9},{11,1... | collective-permute-start | bytes 1327112 | tf_op jit(solution)/shard_map/ppermute | solution.py:29
  115.2 7.1 %copy-start = (bf16[768,1536]{1,0:T(8,128)(2,1)S(1)}, bf16[768,1536]{1,0:T(8,128)(2,1)}, u32[]{:S(2)}) copy-start(bf16[768,1536]{1,0:T(8,128)(2,1)} %param.15) | copy-start | bytes 7077892
  135.2 43.9 %collective-permute-start.15 = (bf16[256,1536]{1,0:T(8,128)(2,1)}, bf16[256,1536]{1,0:T(8,128)(2,1)}, u32[]{:S(2)}, u32[]{:S(2)}) collective-permute-start(bf16[256,1536]{1,0:T(8,128)(2,1)} %slice.184), channel_id=1, source_target_pairs={{0,1},{1,2},{2,3},{3,4},{4,5},{5,6},{6,7},{7,8},{8,9},{9,10},{10,1... | collective-permute-start | bytes 2359304 | tf_op jit(solution)/shard_map/ppermute | solution.py:39
  156.6 8.2 %copy-start.14 = (bf16[256,768]{0,1:T(8,128)(2,1)S(1)}, bf16[256,768]{0,1:T(8,128)(2,1)}, u32[]{:S(2)}) copy-start(bf16[256,768]{0,1:T(8,128)(2,1)} %copy.46) | copy-start | bytes 1179652
  179.1 7.0 %copy-start.13 = (bf16[256,768]{0,1:T(8,128)(2,1)S(1)}, bf16[256,768]{0,1:T(8,128)(2,1)}, u32[]{:S(2)}) copy-start(bf16[256,768]{0,1:T(8,128)(2,1)} %copy.43) | copy-start | bytes 1179652
  205.4 204.7 %all-gather.5.cloned.1.call-start = ((), (), s32[]{:S(2)}) async-start(), calls=%async_computation.3 | async-start | bytes 7520256 | tf_op jit(solution)/shard_map/all_gather | solution.py:179
  206.2 288.6 %reduce-scatter.5.cloned.1.call-start = ((), (), s32[]{:S(2)}) async-start(), calls=%async_computation.4 | async-start | bytes 7520256 | tf_op jit(solution)/shard_map/reduce_scatter | solution.py:168
  206.2 5.5 %copy-start.2 = (bf16[512,768]{0,1:T(8,128)(2,1)S(1)}, bf16[512,768]{0,1:T(8,128)(2,1)}, u32[]{:S(2)}) copy-start(bf16[512,768]{0,1:T(8,128)(2,1)} %copy.48) | copy-start | bytes 2359300
  272.2 23.3 %copy-start.7 = (bf16[256,768]{0,1:T(8,128)(2,1)S(1)}, bf16[256,768]{0,1:T(8,128)(2,1)}, u32[]{:S(2)}) copy-start(bf16[256,768]{0,1:T(8,128)(2,1)} %get-tuple-element.87) | copy-start | bytes 1179652
  272.2 23.3 %copy-start.23 = (f32[12,256]{1,0:T(8,128)S(1)}, f32[12,256]{1,0:T(8,128)}, u32[]{:S(2)}) copy-start(f32[12,256]{1,0:T(8,128)} %get-tuple-element.95) | copy-start | bytes 36868
  299.0 6.8 %slice-start.1 = ((s8[6291456]{0:T(1024)(128)(4,1)}), s8[4194304]{0:T(1024)(128)(4,1)S(1)}, s32[]{:S(2)}) async-start(s8[6291456]{0:T(1024)(128)(4,1)} %bitcast.169), calls=%async_computation.7 | async-start | bytes 8388608
  300.0 5.8 %slice-start.2 = ((s8[6291456]{0:T(1024)(128)(4,1)}), s8[2097152]{0:T(1024)(128)(4,1)S(1)}, s32[]{:S(2)}) async-start(s8[6291456]{0:T(1024)(128)(4,1)} %bitcast.169), calls=%async_computation.8 | async-start | bytes 4194304
  311.4 76.4 %collective-permute-start.16 = (bf16[256,1536]{0,1:T(8,128)(2,1)}, bf16[256,1536]{0,1:T(8,128)(2,1)}, u32[]{:S(2)}, u32[]{:S(2)}) collective-permute-start(bf16[256,1536]{0,1:T(8,128)(2,1)} %slice.212), channel_id=1, source_target_pairs={{1,0},{2,1},{3,2},{4,3},{5,4},{6,5},{7,6},{8,7},{9,8},{10,9},{11,1... | collective-permute-start | bytes 2359304 | tf_op jit(solution)/shard_map/ppermute | solution.py:39
  339.3 22.7 %copy-start.11 = (bf16[512,768]{0,1:T(8,128)(2,1)S(1)}, bf16[512,768]{0,1:T(8,128)(2,1)}, u32[]{:S(2)}) copy-start(bf16[512,768]{0,1:T(8,128)(2,1)} %copy.47) | copy-start | bytes 2359300
  410.2 11.8 %copy-start.5 = (bf16[768,1536]{1,0:T(8,128)(2,1)S(1)}, bf16[768,1536]{1,0:T(8,128)(2,1)}, u32[]{:S(2)}) copy-start(bf16[768,1536]{1,0:T(8,128)(2,1)} %param.20) | copy-start | bytes 7077892
  (16 other events, 50.3 us)
Sparse Core Ops, SparseCore 0:
  26.1 50.4 all-gather.2
  205.6 64.1 reduce-scatter.6
  272.3 70.5 all-gather.4
  401.6 93.1 reduce-scatter.4
